TPU v7x, 32 devices: a whole 2x2x4 slice. The times are simulated.
32 devices in a mesh: row: 4 (over z), col: 8 (over y, x, core).
Axes of the slice: x: 2, y: 2, z: 4, core: 2. Of those that a mesh axis runs over, the one named last changes fastest.
Arguments:
- amplitudes: bfloat16 [16, 16, 12, 4096], P('row', 'col'), may hold values from -6 to 6
- integrals: bfloat16 [16, 16, 47, 4096], P('row', 'col'), may hold values from -0.1875 to 0.1875
- pair_lists: int32 [4, 12, 2], replicated, may hold values from 0 to 46, as said below
- tile_counts: int32 [4], replicated, may hold values from 1 to 12, as said below
Outputs:
- symmetric: float32 [16, 16, 12, 4096], P('row', 'col')
Inputs may be any that keep to these rules, and one draw needn't show every extreme that they name: `pair_lists`: each grid row lists 12 distinct ordered pairs of different tiles. `tile_counts`: the largest count equals 12.
All inputs are finite; a program needn't handle non-finite values.
Results may differ from a plain program's by a relative error of at most 0.0029.
Values may be sent and summed in bfloat16 or wider, within the bound.
No kernel may reach another device: no remote copies, remote signals or barrier semaphores. Data moves between devices by JAX's collectives and lax.ppermute only.
A program may use at most 128 MiB of HBM per device.

v0:
```python
import jax
import jax.numpy as jnp
from jax import lax
from jax.sharding import PartitionSpec as P

TILE = 64


def on_device(amplitudes, integrals, pair_lists, tile_counts):
    occ_row, occ_col, slot_count, square = amplitudes.shape
    tile_width = TILE
    row_devices = lax.axis_size("row")
    col_devices = lax.axis_size("col")
    col_ratio = col_devices // row_devices
    my_row = lax.axis_index("row")
    my_col = lax.axis_index("col")
    partner_row = my_col // col_ratio
    tile_first = pair_lists[:, :, 0]
    tile_second = pair_lists[:, :, 1]
    packed = jnp.take(integrals, tile_second.reshape(-1), axis=2)
    packed = packed.reshape(occ_row, occ_col, row_devices, slot_count, square)
    received = lax.all_to_all(packed, "row", split_axis=2, concat_axis=0, tiled=True)
    received = received.reshape(occ_row * row_devices, occ_col, slot_count, square)
    piece = lax.all_gather(amplitudes, "col", axis=1, tiled=True)
    piece_count = piece.shape[1]
    left_tiles = piece.reshape(occ_row, piece_count, slot_count, tile_width, tile_width)
    right_tiles = received.reshape(piece_count, occ_col, slot_count, tile_width, tile_width)
    cycle_sum = jnp.einsum(
        "iksac,kjscb->ijsab", left_tiles, right_tiles, preferred_element_type=jnp.float32
    )
    my_count = lax.dynamic_index_in_dim(tile_counts, my_row, 0, keepdims=False)
    live_slots = (jnp.arange(slot_count, dtype=jnp.int32) < my_count).astype(jnp.float32)
    cycle_value = (cycle_sum * live_slots[None, None, :, None, None]).astype(jnp.bfloat16)
    cycle = cycle_value.reshape(occ_row, occ_col, slot_count, square)
    residual_strip = lax.all_gather(cycle, "row", axis=0, tiled=True)
    mirror_whole = lax.all_to_all(residual_strip, "col", split_axis=0, concat_axis=1, tiled=True)
    mirror_block = lax.dynamic_slice_in_dim(mirror_whole, my_row * occ_row, occ_row, 1)
    mirror_block = mirror_block.reshape(occ_col, occ_row, slot_count, tile_width, tile_width)
    mine_first = lax.dynamic_index_in_dim(tile_first, my_row, 0, keepdims=False)
    mine_second = lax.dynamic_index_in_dim(tile_second, my_row, 0, keepdims=False)
    their_first = lax.dynamic_index_in_dim(tile_first, partner_row, 0, keepdims=False)
    their_second = lax.dynamic_index_in_dim(tile_second, partner_row, 0, keepdims=False)
    pair_match = (
        (mine_first[:, None] == their_second[None, :])
        & (mine_second[:, None] == their_first[None, :])
    ).astype(jnp.bfloat16)
    crossed = jnp.einsum(
        "st,jitba->ijsab", pair_match, mirror_block, preferred_element_type=jnp.float32
    )
    own_part = cycle_value.astype(jnp.float32)
    symmetric = (own_part + crossed) * live_slots[None, None, :, None, None]
    return symmetric.reshape(occ_row, occ_col, slot_count, square)


def solution(mesh):
    return jax.shard_map(
        on_device,
        mesh=mesh,
        in_specs=(P("row", "col", None, None), P("row", "col", None, None), P(), P()),
        out_specs=P("row", "col", None, None),
        check_vma=False,
    )
```

profile of v0, /device:TPU:0, one launch (start us, length us, event | category | flops | bytes accessed | tf_op | source)
XLA Modules:
  0.0 288.4 jit_solution(7167490492308642510)
XLA Ops:
  6.5 0.0 copy-start
  6.5 0.0 all-gather.3.cloned.1.call-start
  6.5 2.8 copy.17
  9.3 0.0 all-gather.3.cloned.1.call-update
  9.3 0.8 fusion.29
  10.1 0.1 reshape_squeeze.6
  10.2 8.5 %gather_fusion = bf16[48,4,2,4096]{3,2,1,0:T(2,128)(2,1)} fusion(bf16[4,2,47,4096]{3,1,2,0:T(2,128)(2,1)S(1)} %copy-done, s32[1024]{0:T(1024)S(1)} %pad_clamp_fusion), kind=kCustom, calls=%fused_computation | custom fusion | bytes 6291648 | tf_op jit(solution)/shard_map/jit(_take)/gather | solution.py:20
  18.8 6.7 %broadcast_select_fusion = bf16[4,2,4,12,4096]{4,1,3,0,2:T(2,128)(2,1)} fusion(pred[4,12]{1,0:T(4,128)(4,1)S(1)} %compare_and_fusion, bf16[4,2,4,12,4096]{4,1,0,3,2:T(2,128)(2,1)} %bitcast.67), kind=kLoop, calls=%fused_computation.4 | loop fusion | flops 1572864 | bytes 6291504 | tf_op jit(solution)/shard_map/jit(_take)/select_n | solution.py:20
  25.4 6.4 %all-to-all-start = ((bf16[4,2,4,12,4096]{4,1,3,0,2:T(2,128)(2,1)}), bf16[4,2,4,12,4096]{4,1,3,0,2:T(2,128)(2,1)}, u32[]{:S(2)}, u32[]{:S(2)}) async-start(bf16[4,2,4,12,4096]{4,1,3,0,2:T(2,128)(2,1)} %broadcast_select_fusion), calls=%async_computation | async-start | bytes 6291456 | tf_op jit(solution)/shard_map/all_to_all | solution.py:22
  31.9 0.0 all-gather.5.cloned.1.call-start
  31.9 0.6 dynamic_slice.20
  32.5 0.6 compare_convert_fusion
  33.1 69.6 %all-to-all-done = bf16[4,2,4,12,4096]{4,1,3,0,2:T(2,128)(2,1)} async-done(((bf16[4,2,4,12,4096]{4,1,3,0,2:T(2,128)(2,1)}), bf16[4,2,4,12,4096]{4,1,3,0,2:T(2,128)(2,1)}, u32[]{:S(2)}, u32[]{:S(2)}) %all-to-all-start) | async-done | bytes 3145760 | tf_op jit(solution)/shard_map/all_to_all | solution.py:22
  102.7 11.1 %reshape_reshape.3 = bf16[16,2,12,64,64]{4,3,1,2,0:T(8,128)(2,1)} reshape(bf16[4,4,2,1,12,4096]{5,2,4,1,0,3:T(2,128)(2,1)} %bitcast.5) | data formatting | bytes 6291456 | tf_op jit(solution)/shard_map/reshape;reshape | solution.py:27
  113.8 9.4 %copy.18 = bf16[4,16,12,4096]{3,1,0,2:T(8,128)(2,1)} copy(bf16[4,16,12,4096]{3,0,2,1:T(4,128)(2,1)} %all-gather.3.cloned.1.call-done) | data formatting | bytes 12582912 | tf_op jit(solution)/shard_map/all_gather | solution.py:24
  123.2 17.9 %reshape.81 = bf16[4,16,12,64,64,1]{4,3,1,0,2,5:T(8,128)(2,1)} reshape(bf16[4,16,12,4096]{3,1,0,2:T(8,128)(2,1)} %copy.18) | data formatting | bytes 12582912 | tf_op jit(solution)/shard_map/reshape | solution.py:26
  141.1 11.1 %fusion.11 = bf16[4,2,12,64,64]{3,4,0,1,2:T(8,128)(2,1)S(1)} fusion(f32[12]{0:T(128)S(1)} %compare_convert_fusion, bf16[4,16,12,64,64,1]{4,3,1,0,2,5:T(8,128)(2,1)} %reshape.81, bf16[16,2,12,64,64]{4,3,1,2,0:T(8,128)(2,1)} %reshape_reshape.3), kind=kOutput, calls=%fused_computation.11 | convolution fusion | flops 806092800 | bytes 10223664 | tf_op jit(solution)/shard_map/iksac,kjscb->ijsab/dot_general | solution.py:28
  152.2 1.7 copy.20
  153.9 3.9 %reshape.69 = bf16[4,2,12,4096]{3,1,2,0:T(2,128)(2,1)} reshape(bf16[4,2,12,64,64]{4,3,1,2,0:T(8,128)(2,1)} %copy.20) | data formatting | bytes 1572864 | tf_op jit(solution)/shard_map/reshape | solution.py:34
  157.7 0.0 all-gather.5.cloned.1.call-update
  157.8 0.0 copy-done.2
  157.8 62.7 %all-gather.5.cloned.1.call-done = bf16[16,2,12,4096]{3,1,2,0:T(2,128)(2,1)} async-done(((bf16[4,2,12,4096]{3,1,2,0:T(2,128)(2,1)}), bf16[16,2,12,4096]{3,1,2,0:T(2,128)(2,1)}) %all-gather.5.cloned.1.call-update) | async-done | bytes 3145744 | tf_op jit(solution)/shard_map/all_gather | solution.py:35
  220.4 4.7 %all-to-all-start.1 = ((bf16[16,2,12,4096]{3,1,2,0:T(2,128)(2,1)}), bf16[16,2,12,4096]{3,1,2,0:T(2,128)(2,1)}, u32[]{:S(2)}, u32[]{:S(2)}) async-start(bf16[16,2,12,4096]{3,1,2,0:T(2,128)(2,1)} %all-gather.5.cloned.1.call-done), calls=%async_computation.1 | async-start | bytes 6291456 | tf_op jit(solution)/shard_map/all_to_all | solution.py:36
  225.2 37.6 %all-to-all-done.1 = bf16[16,2,12,4096]{3,1,2,0:T(2,128)(2,1)} async-done(((bf16[16,2,12,4096]{3,1,2,0:T(2,128)(2,1)}), bf16[16,2,12,4096]{3,1,2,0:T(2,128)(2,1)}, u32[]{:S(2)}, u32[]{:S(2)}) %all-to-all-start.1) | async-done | bytes 3145760 | tf_op jit(solution)/shard_map/all_to_all | solution.py:36
  262.8 5.1 %copy.21 = bf16[8,2,2,12,4096]{4,1,3,2,0:T(2,128)(2,1)S(1)} copy(bf16[8,2,2,12,4096]{4,2,3,1,0:T(2,128)(2,1)} %bitcast.12) | data formatting | bytes 6291456 | tf_op jit(solution)/shard_map/all_to_all | solution.py:36
  267.9 0.7 constant_dynamic-slice_fusion.4
  268.6 1.0 reshape.85
  269.6 1.1 fusion.5
  270.7 0.3 copy-done.3
  271.0 2.7 fusion.3
  273.7 3.7 %copy.25 = f32[4,2,12,64,64]{4,3,1,2,0:T(8,128)} copy(f32[4,2,12,64,64]{3,4,0,1,2:T(8,128)} %fusion.3) | data formatting | bytes 3145728 | tf_op jit(solution)/shard_map/mul | solution.py:51
  277.4 4.2 %reshape.71 = f32[4,2,12,4096]{3,1,2,0:T(2,128)} reshape(f32[4,2,12,64,64]{4,3,1,2,0:T(8,128)} %copy.25) | data formatting | bytes 3145728 | tf_op jit(solution)/shard_map/reshape | solution.py:52
  (12 shorter events, 0.0 us)
Async XLA Ops:
  6.5 3.7 %copy-start = (bf16[4,2,47,4096]{3,1,2,0:T(2,128)(2,1)S(1)}, bf16[4,2,47,4096]{3,1,2,0:T(2,128)(2,1)}, u32[]{:S(2)}) copy-start(bf16[4,2,47,4096]{3,1,2,0:T(2,128)(2,1)} %param.5) | copy-start | bytes 9240580
  6.5 107.3 %all-gather.3.cloned.1.call-start = ((), (), s32[]{:S(2)}) async-start(), calls=%async_computation.2 | async-start | bytes 7077888 | tf_op jit(solution)/shard_map/all_gather | solution.py:24
  25.4 6.4 %copy-start.4 = (s32[4]{0:T(128)S(1)}, s32[4]{0:T(128)}, u32[]{:S(2)}) copy-start(s32[4]{0:T(128)} %param.7) | copy-start | bytes 52
  25.4 77.3 %all-to-all-start = ((bf16[4,2,4,12,4096]{4,1,3,0,2:T(2,128)(2,1)}), bf16[4,2,4,12,4096]{4,1,3,0,2:T(2,128)(2,1)}, u32[]{:S(2)}, u32[]{:S(2)}) async-start(bf16[4,2,4,12,4096]{4,1,3,0,2:T(2,128)(2,1)} %broadcast_select_fusion), calls=%async_computation | async-start | bytes 6291456 | tf_op jit(solution)/shard_map/all_to_all | solution.py:22
  31.9 188.6 %all-gather.5.cloned.1.call-start = ((), (), s32[]{:S(2)}) async-start(), calls=%async_computation.3 | async-start | bytes 3932160 | tf_op jit(solution)/shard_map/all_gather | solution.py:35
  152.2 5.6 %copy-start.2 = (bf16[4,2,12,64,64]{3,4,0,1,2:T(8,128)(2,1)}, bf16[4,2,12,64,64]{3,4,0,1,2:T(8,128)(2,1)S(1)}, u32[]{:S(2)}) copy-start(bf16[4,2,12,64,64]{3,4,0,1,2:T(8,128)(2,1)S(1)} %fusion.11) | copy-start | bytes 2359300
  220.4 42.3 %all-to-all-start.1 = ((bf16[16,2,12,4096]{3,1,2,0:T(2,128)(2,1)}), bf16[16,2,12,4096]{3,1,2,0:T(2,128)(2,1)}, u32[]{:S(2)}, u32[]{:S(2)}) async-start(bf16[16,2,12,4096]{3,1,2,0:T(2,128)(2,1)} %all-gather.5.cloned.1.call-done), calls=%async_computation.1 | async-start | bytes 6291456 | tf_op jit(solution)/shard_map/all_to_all | solution.py:36
  269.6 1.4 copy-start.3
  273.7 7.9 %copy-start.1 = (bf16[4,2,47,4096]{3,1,2,0:T(2,128)(2,1)S(1)}, bf16[4,2,47,4096]{3,1,2,0:T(2,128)(2,1)}, u32[]{:S(2)}) copy-start(bf16[4,2,47,4096]{3,1,2,0:T(2,128)(2,1)} %param.5) | copy-start | bytes 9240580
Sparse Core Ops, SparseCore 0:
  9.5 48.1 all-gather.2
  157.9 62.5 all-gather.4
where the time goes:
time: 290 us; the launch traced here: 288 us
  waiting for transfers between devices  170 us (59%)
  local copies, waits for them, and re-layouts  71.7 us (25%)
  between operations  13.5 us (5%)
  matrix products  12.2 us (4%)
  starting transfers between devices  11.1 us (4%)
  other arithmetic  10 us (3%)
    all_to_all x1, waiting for transfers between devices, on_device(): lax.all_to_all(packed, 'row', split_axis=2, concat_axis=0, tiled=True)  69.6 us
    all_gather x1, waiting for transfers between devices, on_device(): residual_strip = lax.all_gather(cycle, 'row', axis=0, tiled=True)  62.7 us
    all_to_all x1, waiting for transfers between devices, on_device(): lax.all_to_all(residual_strip, 'col', split_axis=0, concat_axis=1, tiled=...  37.6 us
    reshape x1, local copies, waits for them, and re-layouts, on_device(): piece.reshape(occ_row, piece_count, slot_count, tile_width, tile_width)  17.9 us
    another operation x1, local copies, waits for them, and re-layouts, on_device(): received.reshape(piece_count, occ_col, slot_count, tile_width, tile_width)  11.1 us
    dot_general x1, matrix products, on_device(): jnp.einsum('iksac,kjscb->ijsab', left_tiles, right_tiles, preferred_eleme...  11.1 us
    all_gather x1, local copies, waits for them, and re-layouts, on_device(): piece = lax.all_gather(amplitudes, 'col', axis=1, tiled=True)  9.35 us
    gather x1, local copies, waits for them, and re-layouts, on_device(): packed = jnp.take(integrals, tile_second.reshape(-1), axis=2)  8.51 us
  transfers between devices with their start and end apart: 4, of which 3 were waited for; matrix products, arithmetic and copies ran while one was open for 10% of the time, Pallas kernels for 0%

commit v1 on v0

--- a/solution.py
+++ b/solution.py
@@ -2,6 +2,7 @@
 import jax.numpy as jnp
 from jax import lax
 from jax.sharding import PartitionSpec as P
+from jax.lax import axis_index, axis_size, ppermute
 
 TILE = 64
 
@@ -32,7 +33,17 @@
     live_slots = (jnp.arange(slot_count, dtype=jnp.int32) < my_count).astype(jnp.float32)
     cycle_value = (cycle_sum * live_slots[None, None, :, None, None]).astype(jnp.bfloat16)
     cycle = cycle_value.reshape(occ_row, occ_col, slot_count, square)
-    residual_strip = lax.all_gather(cycle, "row", axis=0, tiled=True)
+    n_all = axis_size("row")
+    gallery = [cycle]
+    for s in range(n_all - 1):
+        gallery.append(
+            ppermute(gallery[-1], "row", [(dd, (dd + 1) % n_all) for dd in range(n_all)])
+        )
+    residual_strip = jnp.roll(
+        jnp.concatenate(gallery[::-1], axis=0),
+        shift=(axis_index("row") + 1) * cycle.shape[0],
+        axis=0,
+    )
     mirror_whole = lax.all_to_all(residual_strip, "col", split_axis=0, concat_axis=1, tiled=True)
     mirror_block = lax.dynamic_slice_in_dim(mirror_whole, my_row * occ_row, occ_row, 1)
     mirror_block = mirror_block.reshape(occ_col, occ_row, slot_count, tile_width, tile_width)

time: 290 us -> 300 us (1.034)
  local copies, waits for them, and re-layouts: 71.7 us -> 86.3 us
  waiting for transfers between devices: 170 us -> 166 us
    all_gather x1 -> x0, waiting for transfers between devices: 62.7 us -> none  [on_device(): residual_strip = lax.all_gather(cycle, 'row', axis=0, tiled=True)]
    ppermute x0 -> x3, waiting for transfers between devices: none -> 58.3 us  [on_device(): ppermute(gallery[-1], 'row', [(dd, (dd + 1) % n_all) for dd in range(n_al...]
    unnamed x11 -> x18, local copies, waits for them, and re-layouts: 3.1 us -> 13 us
    dynamic_slice x0 -> x1, local copies, waits for them, and re-layouts: none -> 4.73 us  [on_device(): jnp.roll(jnp.concatenate(gallery[::-1], axis=0), shift=(axis_index('row')...]
  transfers between devices with their start and end apart: 4 -> 6, of which waited for: 3 -> 5; matrix products, arithmetic and copies ran while one was open for 10% -> 10% of each run, Pallas kernels for 0% -> 0%
where the time goes in v1:
time: 300 us; the launch traced here: 299 us
  waiting for transfers between devices  166 us (55%)
  local copies, waits for them, and re-layouts  86.3 us (29%)
  between operations  13.6 us (5%)
  matrix products  12.2 us (4%)
  starting transfers between devices  11.2 us (4%)
  other arithmetic  10 us (3%)
    all_to_all x1, waiting for transfers between devices, on_device(): lax.all_to_all(packed, 'row', split_axis=2, concat_axis=0, tiled=True)  69.8 us
    ppermute x3, waiting for transfers between devices, on_device(): ppermute(gallery[-1], 'row', [(dd, (dd + 1) % n_all) for dd in range(n_al...  58.3 us
    all_to_all x1, waiting for transfers between devices, on_device(): lax.all_to_all(residual_strip, 'col', split_axis=0, concat_axis=1, tiled=...  37.6 us
    reshape x1, local copies, waits for them, and re-layouts, on_device(): piece.reshape(occ_row, piece_count, slot_count, tile_width, tile_width)  17.9 us
    unnamed x18, local copies, waits for them, and re-layouts  13 us
    another operation x1, local copies, waits for them, and re-layouts, on_device(): received.reshape(piece_count, occ_col, slot_count, tile_width, tile_width)  11.1 us
    dot_general x1, matrix products, on_device(): jnp.einsum('iksac,kjscb->ijsab', left_tiles, right_tiles, preferred_eleme...  11.1 us
    all_gather x1, local copies, waits for them, and re-layouts, on_device(): piece = lax.all_gather(amplitudes, 'col', axis=1, tiled=True)  9.35 us
  transfers between devices with their start and end apart: 6, of which 5 were waited for; matrix products, arithmetic and copies ran while one was open for 10% of the time, Pallas kernels for 0%

profile of v1, /device:TPU:0, one launch (start us, length us, event | category | flops | bytes accessed | tf_op | source)
XLA Modules:
  0.0 298.9 jit_solution(12801907893527067175)
XLA Ops:
  6.5 2.8 copy.17
  10.2 8.5 %gather_fusion = bf16[48,4,2,4096]{3,2,1,0:T(2,128)(2,1)} fusion(bf16[4,2,47,4096]{3,1,2,0:T(2,128)(2,1)S(1)} %copy-done, s32[1024]{0:T(1024)S(1)} %pad_clamp_fusion), kind=kCustom, calls=%fused_computation | custom fusion | bytes 6291648 | tf_op jit(solution)/shard_map/jit(_take)/gather | solution.py:21
  18.8 6.7 %broadcast_select_fusion = bf16[4,2,4,12,4096]{4,1,3,0,2:T(2,128)(2,1)} fusion(pred[4,12]{1,0:T(4,128)(4,1)S(1)} %compare_and_fusion, bf16[4,2,4,12,4096]{4,1,0,3,2:T(2,128)(2,1)} %bitcast.67), kind=kLoop, calls=%fused_computation.4 | loop fusion | flops 1572864 | bytes 6291504 | tf_op jit(solution)/shard_map/jit(_take)/select_n | solution.py:21
  25.4 6.4 %all-to-all-start = ((bf16[4,2,4,12,4096]{4,1,3,0,2:T(2,128)(2,1)}), bf16[4,2,4,12,4096]{4,1,3,0,2:T(2,128)(2,1)}, u32[]{:S(2)}, u32[]{:S(2)}) async-start(bf16[4,2,4,12,4096]{4,1,3,0,2:T(2,128)(2,1)} %broadcast_select_fusion), calls=%async_computation | async-start | bytes 6291456 | tf_op jit(solution)/shard_map/all_to_all | solution.py:23
  33.1 69.8 %all-to-all-done = bf16[4,2,4,12,4096]{4,1,3,0,2:T(2,128)(2,1)} async-done(((bf16[4,2,4,12,4096]{4,1,3,0,2:T(2,128)(2,1)}), bf16[4,2,4,12,4096]{4,1,3,0,2:T(2,128)(2,1)}, u32[]{:S(2)}, u32[]{:S(2)}) %all-to-all-start) | async-done | bytes 3145760 | tf_op jit(solution)/shard_map/all_to_all | solution.py:23
  102.9 11.1 %reshape_reshape.3 = bf16[16,2,12,64,64]{4,3,1,2,0:T(8,128)(2,1)} reshape(bf16[4,4,2,1,12,4096]{5,2,4,1,0,3:T(2,128)(2,1)} %bitcast.5) | data formatting | bytes 6291456 | tf_op jit(solution)/shard_map/reshape;reshape | solution.py:28
  114.0 9.4 %copy.18 = bf16[4,16,12,4096]{3,1,0,2:T(8,128)(2,1)} copy(bf16[4,16,12,4096]{3,0,2,1:T(4,128)(2,1)} %all-gather.2.cloned.1.call-done) | data formatting | bytes 12582912 | tf_op jit(solution)/shard_map/all_gather | solution.py:25
  123.4 17.9 %reshape.81 = bf16[4,16,12,64,64,1]{4,3,1,0,2,5:T(8,128)(2,1)} reshape(bf16[4,16,12,4096]{3,1,0,2:T(8,128)(2,1)} %copy.18) | data formatting | bytes 12582912 | tf_op jit(solution)/shard_map/reshape | solution.py:27
  141.3 11.1 %fusion.11 = bf16[4,2,12,64,64]{3,4,0,1,2:T(8,128)(2,1)S(1)} fusion(f32[12]{0:T(128)S(1)} %compare_convert_fusion, bf16[4,16,12,64,64,1]{4,3,1,0,2,5:T(8,128)(2,1)} %reshape.81, bf16[16,2,12,64,64]{4,3,1,2,0:T(8,128)(2,1)} %reshape_reshape.3), kind=kOutput, calls=%fused_computation.11 | convolution fusion | flops 806092800 | bytes 10223664 | tf_op jit(solution)/shard_map/iksac,kjscb->ijsab/dot_general | solution.py:29
  152.4 1.1 copy-done.2
  153.5 1.6 copy.20
  155.1 3.1 %reshape.69 = bf16[4,2,12,4096]{3,1,2,0:T(2,128)(2,1)S(1)} reshape(bf16[4,2,12,64,64]{4,3,1,2,0:T(8,128)(2,1)} %copy.20) | data formatting | bytes 1572864 | tf_op jit(solution)/shard_map/reshape | solution.py:35
  158.3 20.2 %collective-permute-done = bf16[4,2,12,4096]{3,1,2,0:T(2,128)(2,1)S(1)} collective-permute-done((bf16[4,2,12,4096]{3,1,2,0:T(2,128)(2,1)S(1)}, bf16[4,2,12,4096]{3,1,2,0:T(2,128)(2,1)S(1)}, u32[]{:S(2)}, u32[]{:S(2)}) %collective-permute-start) | collective-permute-done | bytes 786464 | tf_op jit(solution)/shard_map/ppermute | solution.py:40
  178.5 19.4 %collective-permute-done.1 = bf16[4,2,12,4096]{3,1,2,0:T(2,128)(2,1)S(1)} collective-permute-done((bf16[4,2,12,4096]{3,1,2,0:T(2,128)(2,1)S(1)}, bf16[4,2,12,4096]{3,1,2,0:T(2,128)(2,1)S(1)}, u32[]{:S(2)}, u32[]{:S(2)}) %collective-permute-start.1) | collective-permute-done | bytes 786464 | tf_op jit(solution)/shard_map/ppermute | solution.py:40
  197.9 18.6 %collective-permute-done.2 = bf16[4,2,12,4096]{3,1,2,0:T(2,128)(2,1)} collective-permute-done((bf16[4,2,12,4096]{3,1,2,0:T(2,128)(2,1)S(1)}, bf16[4,2,12,4096]{3,1,2,0:T(2,128)(2,1)}, u32[]{:S(2)}, u32[]{:S(2)}) %collective-permute-start.2) | collective-permute-done | bytes 786464 | tf_op jit(solution)/shard_map/ppermute | solution.py:40
  216.5 1.8 constant_dynamic-update-slice_fusion.7
  218.3 1.0 constant_dynamic-update-slice_fusion.6
  219.3 1.0 constant_dynamic-update-slice_fusion.5
  220.3 1.0 constant_dynamic-update-slice_fusion.4
  221.3 2.1 constant_dynamic-update-slice_fusion.3
  223.4 1.0 constant_dynamic-update-slice_fusion.2
  224.4 1.0 constant_dynamic-update-slice_fusion.1
  225.3 1.0 constant_dynamic-update-slice_fusion
  226.3 4.7 %constant_dynamic-slice_fusion.5 = bf16[16,2,12,4096]{3,1,2,0:T(2,128)(2,1)} fusion(bf16[32,2,12,4096]{3,1,2,0:T(2,128)(2,1)S(1)} %constant_dynamic-update-slice_fusion, s32[]{:T(128)S(6)} %select_n.58), kind=kLoop, calls=%fused_computation.38 | loop fusion | bytes 6291460 | tf_op jit(solution)/shard_map/jit(_roll_dynamic)/dynamic_slice | solution.py:42
  231.0 4.7 %all-to-all-start.1 = ((bf16[16,2,12,4096]{3,1,2,0:T(2,128)(2,1)}), bf16[16,2,12,4096]{3,1,2,0:T(2,128)(2,1)}, u32[]{:S(2)}, u32[]{:S(2)}) async-start(bf16[16,2,12,4096]{3,1,2,0:T(2,128)(2,1)} %constant_dynamic-slice_fusion.5), calls=%async_computation.1 | async-start | bytes 6291456 | tf_op jit(solution)/shard_map/all_to_all | solution.py:47
  235.8 37.6 %all-to-all-done.1 = bf16[16,2,12,4096]{3,1,2,0:T(2,128)(2,1)} async-done(((bf16[16,2,12,4096]{3,1,2,0:T(2,128)(2,1)}), bf16[16,2,12,4096]{3,1,2,0:T(2,128)(2,1)}, u32[]{:S(2)}, u32[]{:S(2)}) %all-to-all-start.1) | async-done | bytes 3145760 | tf_op jit(solution)/shard_map/all_to_all | solution.py:47
  273.4 5.1 %copy.21 = bf16[8,2,2,12,4096]{4,1,3,2,0:T(2,128)(2,1)S(1)} copy(bf16[8,2,2,12,4096]{4,2,3,1,0:T(2,128)(2,1)} %bitcast.12) | data formatting | bytes 6291456 | tf_op jit(solution)/shard_map/all_to_all | solution.py:47
  279.2 1.0 reshape.85
  280.2 1.1 fusion.5
  281.6 2.7 fusion.3
  284.3 3.6 %copy.25 = f32[4,2,12,64,64]{4,3,1,2,0:T(8,128)} copy(f32[4,2,12,64,64]{3,4,0,1,2:T(8,128)} %fusion.3) | data formatting | bytes 3145728 | tf_op jit(solution)/shard_map/mul | solution.py:62
  287.9 4.2 %reshape.71 = f32[4,2,12,4096]{3,1,2,0:T(2,128)} reshape(f32[4,2,12,64,64]{4,3,1,2,0:T(8,128)} %copy.25) | data formatting | bytes 3145728 | tf_op jit(solution)/shard_map/reshape | solution.py:63
  (24 shorter events, 3.2 us)
Async XLA Ops:
  6.5 3.7 %copy-start = (bf16[4,2,47,4096]{3,1,2,0:T(2,128)(2,1)S(1)}, bf16[4,2,47,4096]{3,1,2,0:T(2,128)(2,1)}, u32[]{:S(2)}) copy-start(bf16[4,2,47,4096]{3,1,2,0:T(2,128)(2,1)} %param.5) | copy-start | bytes 9240580
  6.5 107.5 %all-gather.2.cloned.1.call-start = ((), (), s32[]{:S(2)}) async-start(), calls=%async_computation.2 | async-start | bytes 7077888 | tf_op jit(solution)/shard_map/all_gather | solution.py:25
  25.4 6.4 %copy-start.4 = (s32[4]{0:T(128)S(1)}, s32[4]{0:T(128)}, u32[]{:S(2)}) copy-start(s32[4]{0:T(128)} %param.7) | copy-start | bytes 52
  25.4 77.5 %all-to-all-start = ((bf16[4,2,4,12,4096]{4,1,3,0,2:T(2,128)(2,1)}), bf16[4,2,4,12,4096]{4,1,3,0,2:T(2,128)(2,1)}, u32[]{:S(2)}, u32[]{:S(2)}) async-start(bf16[4,2,4,12,4096]{4,1,3,0,2:T(2,128)(2,1)} %broadcast_select_fusion), calls=%async_computation | async-start | bytes 6291456 | tf_op jit(solution)/shard_map/all_to_all | solution.py:23
  152.4 1.2 copy-start.2
  158.2 20.3 %collective-permute-start = (bf16[4,2,12,4096]{3,1,2,0:T(2,128)(2,1)S(1)}, bf16[4,2,12,4096]{3,1,2,0:T(2,128)(2,1)S(1)}, u32[]{:S(2)}, u32[]{:S(2)}) collective-permute-start(bf16[4,2,12,4096]{3,1,2,0:T(2,128)(2,1)S(1)} %reshape.69), channel_id=1, source_target_pairs={{0,8},{8,16},{16,24},{24,0},{1,9},{9,17},{17,25},{25,1},{2,10},{10... | collective-permute-start | bytes 2359304 | tf_op jit(solution)/shard_map/ppermute | solution.py:40
  178.5 19.4 %collective-permute-start.1 = (bf16[4,2,12,4096]{3,1,2,0:T(2,128)(2,1)S(1)}, bf16[4,2,12,4096]{3,1,2,0:T(2,128)(2,1)S(1)}, u32[]{:S(2)}, u32[]{:S(2)}) collective-permute-start(bf16[4,2,12,4096]{3,1,2,0:T(2,128)(2,1)S(1)} %collective-permute-done), channel_id=1, source_target_pairs={{0,8},{8,16},{16,24},{24,0},{1,9},{9,17},{17,25},{25,1},{2,10},{10... | collective-permute-start | bytes 2359304 | tf_op jit(solution)/shard_map/ppermute | solution.py:40
  197.9 18.6 %collective-permute-start.2 = (bf16[4,2,12,4096]{3,1,2,0:T(2,128)(2,1)S(1)}, bf16[4,2,12,4096]{3,1,2,0:T(2,128)(2,1)}, u32[]{:S(2)}, u32[]{:S(2)}) collective-permute-start(bf16[4,2,12,4096]{3,1,2,0:T(2,128)(2,1)S(1)} %collective-permute-done.1), channel_id=1, source_target_pairs={{0,8},{8,16},{16,24},{24,0},{1,9},{9,17},{17,25},{25,1},{2,10},{10... | collective-permute-start | bytes 2359304 | tf_op jit(solution)/shard_map/ppermute | solution.py:40
  231.0 42.3 %all-to-all-start.1 = ((bf16[16,2,12,4096]{3,1,2,0:T(2,128)(2,1)}), bf16[16,2,12,4096]{3,1,2,0:T(2,128)(2,1)}, u32[]{:S(2)}, u32[]{:S(2)}) async-start(bf16[16,2,12,4096]{3,1,2,0:T(2,128)(2,1)} %constant_dynamic-slice_fusion.5), calls=%async_computation.1 | async-start | bytes 6291456 | tf_op jit(solution)/shard_map/all_to_all | solution.py:47
  280.2 1.4 copy-start.3
  281.6 10.4 %copy-start.1 = (bf16[4,2,47,4096]{3,1,2,0:T(2,128)(2,1)S(1)}, bf16[4,2,47,4096]{3,1,2,0:T(2,128)(2,1)}, u32[]{:S(2)}) copy-start(bf16[4,2,47,4096]{3,1,2,0:T(2,128)(2,1)} %param.5) | copy-start | bytes 9240580
Sparse Core Ops, SparseCore 0:
  9.5 48.1 all-gather.1
